TPU v7x, 128 devices: a whole 4x4x4 slice. The times are simulated.
128 devices in a mesh: seq: 4 (over z_lo, core), res: 32 (over y, x, z_hi).
Axes of the slice: x: 4, y: 4, z: 4 (z_hi: 2, z_lo: 2; z = z_hi * 2 + z_lo), core: 2. Of those that a mesh axis runs over, the one named last changes fastest.
Arguments:
- homolog_embedding: bfloat16 [16, 2048, 256], P('seq', 'res'), may hold values from -6 to 6
- pair_input_rows: bfloat16 [2048, 2048, 128], P('res', 'seq'), may hold values from -256 to 256
- incoming_slope: bfloat16 [16, 2048, 256], P('seq', 'res'), may hold values from -6 to 6
- rescale_factor: float32 [256], replicated, may hold values from 0.25 to 1.75
- probe_weights: bfloat16 [256, 256], replicated, may hold values from -0.375 to 0.375
- lookup_weights: bfloat16 [256, 256], replicated, may hold values from -0.375 to 0.375
- content_weights: bfloat16 [256, 256], replicated, may hold values from -0.375 to 0.375
- sigmoid_weights: bfloat16 [256, 256], replicated, may hold values from -0.375 to 0.375
- final_projection: bfloat16 [256, 256], replicated, may hold values from -0.375 to 0.375
- pair_bias_matrix: bfloat16 [128, 8], replicated, may hold values from -1 to 1
Outputs:
- alignment_rows_gradient: bfloat16 [16, 2048, 256], P('seq', 'res')
- pair_input_gradient: bfloat16 [2048, 2048, 128], P('res', 'seq')
- layer_gain_gradient: float32 [256], replicated
- query_matrix_gradient: float32 [256, 256], replicated
- key_matrix_gradient: float32 [256, 256], replicated
- value_matrix_gradient: float32 [256, 256], replicated
- gate_matrix_gradient: float32 [256, 256], replicated
- final_projection_slope: float32 [256, 256], replicated
- pair_bias_matrix_gradient: float32 [128, 8], replicated
All inputs are finite; a program needn't handle non-finite values.
Results may differ from a plain program's by a relative error of at most 0.0034.
The roundings to bfloat16 on the way count: a program that leaves them out, or rounds other values in their place, can miss the bound.
Values may be sent and summed in bfloat16 or wider, within the bound.
A program may use at most 128 MiB of HBM per device.

v0:
```python
import functools
import math
import jax
import jax.numpy as jnp
from jax import lax
from jax.sharding import PartitionSpec as P


def layer_norm_rows(alignment_block):
    content_vectors = alignment_block.astype(jnp.float32)
    centered = content_vectors - jnp.mean(content_vectors, axis=-1, keepdims=True)
    inverse_deviation = lax.rsqrt(jnp.mean(centered * centered, axis=-1, keepdims=True) + 1e-05)
    return (centered * inverse_deviation, inverse_deviation)


def row_backward(bias_full, head_count, dbias_total, row_inputs):
    probe_vectors, keys_row, values_row, gate_row, derivative_modulated = row_inputs
    query_total, channel_width = probe_vectors.shape
    key_count = keys_row.shape[0]
    head_width = channel_width // head_count
    softmax_scale = 1.0 / math.sqrt(head_width)
    query_heads = probe_vectors.reshape(query_total, head_count, head_width)
    key_heads = keys_row.reshape(key_count, head_count, head_width)
    value_heads = values_row.reshape(key_count, head_count, head_width)
    scores = (
        jnp.einsum("ihd,jhd->hij", query_heads, key_heads, preferred_element_type=jnp.float32)
        * softmax_scale
    )
    scores = scores + bias_full.astype(jnp.float32)
    weights_soft = jax.nn.softmax(scores, axis=-1)
    weights_half = weights_soft.astype(jnp.bfloat16)
    attended = jnp.einsum(
        "hij,jhd->ihd", weights_half, value_heads, preferred_element_type=jnp.float32
    ).reshape(query_total, channel_width)
    modulated_result = (gate_row * attended).astype(jnp.bfloat16)
    grad_attended = (derivative_modulated * gate_row).astype(jnp.bfloat16)
    derivative_logits_sigmoid = (
        derivative_modulated * attended * gate_row * (1.0 - gate_row)
    ).astype(jnp.bfloat16)
    grad_heads = grad_attended.reshape(query_total, head_count, head_width)
    grad_weights = jnp.einsum(
        "ihd,jhd->hij", grad_heads, value_heads, preferred_element_type=jnp.float32
    )
    row_inner = jnp.sum(weights_soft * grad_weights, axis=-1, keepdims=True)
    grad_scores = weights_soft * (grad_weights - row_inner)
    scores_half = grad_scores.astype(jnp.bfloat16)
    derivative_probe_weights = (
        jnp.einsum("hij,jhd->ihd", scores_half, key_heads, preferred_element_type=jnp.float32)
        * softmax_scale
    ).astype(jnp.bfloat16)
    derivative_lookup_weights = (
        jnp.einsum("hij,ihd->jhd", scores_half, query_heads, preferred_element_type=jnp.float32)
        * softmax_scale
    )
    derivative_content_weights = jnp.einsum(
        "hij,ihd->jhd", weights_half, grad_heads, preferred_element_type=jnp.float32
    )
    outputs = (
        modulated_result,
        derivative_logits_sigmoid,
        derivative_probe_weights.reshape(query_total, channel_width),
        derivative_lookup_weights.reshape(key_count, channel_width),
        derivative_content_weights.reshape(key_count, channel_width),
    )
    return (dbias_total + grad_scores, outputs)


def body(
    homolog_embedding,
    pair_input_rows,
    incoming_slope,
    rescale_factor,
    probe_weights,
    lookup_weights,
    content_weights,
    sigmoid_weights,
    final_projection,
    pair_bias_matrix,
):
    highest = lax.Precision.HIGHEST
    head_count = pair_bias_matrix.shape[1]
    row_total, query_total, channel_width = homolog_embedding.shape
    standardized_rows, inverse_deviation = layer_norm_rows(homolog_embedding)
    rescaled_embedding = (standardized_rows * rescale_factor).astype(jnp.bfloat16)
    rescaled_plain = rescaled_embedding.reshape(-1, channel_width)
    probe_vectors = (
        jnp.dot(rescaled_plain, probe_weights, preferred_element_type=jnp.float32)
        .astype(jnp.bfloat16)
        .reshape(row_total, query_total, channel_width)
    )
    sigmoid_factors = jax.nn.sigmoid(
        jnp.dot(rescaled_plain, sigmoid_weights, preferred_element_type=jnp.float32)
    ).reshape(row_total, query_total, channel_width)
    incoming_slope_plain = incoming_slope.reshape(-1, channel_width)
    derivative_modulated = jnp.dot(
        incoming_slope_plain, final_projection.T, preferred_element_type=jnp.float32
    ).reshape(row_total, query_total, channel_width)
    bias_local = jnp.einsum(
        "ijc,ch->hij", pair_input_rows, pair_bias_matrix, preferred_element_type=jnp.float32
    ).astype(jnp.bfloat16)
    bias_full = lax.all_gather(bias_local, "seq", axis=2, tiled=True)
    normed_all = lax.all_gather(rescaled_embedding, "res", axis=1, tiled=True)
    key_count = normed_all.shape[1]
    all_flat = normed_all.reshape(-1, channel_width)
    lookup_vectors = (
        jnp.dot(all_flat, lookup_weights, preferred_element_type=jnp.float32)
        .astype(jnp.bfloat16)
        .reshape(row_total, key_count, channel_width)
    )
    content_vectors = (
        jnp.dot(all_flat, content_weights, preferred_element_type=jnp.float32)
        .astype(jnp.bfloat16)
        .reshape(row_total, key_count, channel_width)
    )
    dbias_init = jnp.zeros(bias_full.shape, jnp.float32)
    dbias_local, row_results = lax.scan(
        functools.partial(row_backward, bias_full, head_count),
        dbias_init,
        (probe_vectors, lookup_vectors, content_vectors, sigmoid_factors, derivative_modulated),
    )
    (
        modulated_result,
        derivative_logits_sigmoid,
        derivative_probe_weights,
        derivative_lookup_weights,
        derivative_content_weights,
    ) = row_results
    key_weight_wide = lookup_weights.astype(jnp.float32)
    value_weight_wide = content_weights.astype(jnp.float32)
    lookup_plain = derivative_lookup_weights.reshape(-1, channel_width)
    content_plain = derivative_content_weights.reshape(-1, channel_width)
    key_term = (
        jnp.dot(lookup_plain, key_weight_wide.T, precision=highest)
        + jnp.dot(content_plain, value_weight_wide.T, precision=highest)
    ).reshape(row_total, -1, channel_width)
    grad_from_keys = lax.psum_scatter(key_term, "res", scatter_dimension=1, tiled=True).reshape(
        -1, channel_width
    )
    all_wide = all_flat.astype(jnp.float32)
    part_key = jnp.dot(all_wide.T, lookup_plain, precision=highest)
    part_value = jnp.dot(all_wide.T, content_plain, precision=highest)
    probe_plain = derivative_probe_weights.reshape(-1, channel_width)
    sigmoid_factor_plain = derivative_logits_sigmoid.reshape(-1, channel_width)
    part_query = jnp.dot(rescaled_plain.T, probe_plain, preferred_element_type=jnp.float32)
    part_gate = jnp.dot(rescaled_plain.T, sigmoid_factor_plain, preferred_element_type=jnp.float32)
    part_out = jnp.dot(
        modulated_result.reshape(-1, channel_width).T,
        incoming_slope_plain,
        preferred_element_type=jnp.float32,
    )
    derivative_rescaled = (
        jnp.dot(probe_plain, probe_weights.T, preferred_element_type=jnp.float32)
        + jnp.dot(sigmoid_factor_plain, sigmoid_weights.T, preferred_element_type=jnp.float32)
        + grad_from_keys
    )
    derivative_rescaled = derivative_rescaled.reshape(row_total, query_total, channel_width)
    part_gain = jnp.sum(derivative_rescaled * standardized_rows, axis=(0, 1))
    centered_scaled_gradient = derivative_rescaled * rescale_factor
    alignment_rows_gradient = (
        inverse_deviation
        * (
            centered_scaled_gradient
            - jnp.mean(centered_scaled_gradient, axis=-1, keepdims=True)
            - standardized_rows
            * jnp.mean(centered_scaled_gradient * standardized_rows, axis=-1, keepdims=True)
        )
    ).astype(jnp.bfloat16)
    dbias_own = lax.psum_scatter(dbias_local, "seq", scatter_dimension=2, tiled=True).astype(
        jnp.bfloat16
    )
    pair_input_gradient = jnp.einsum(
        "hij,ch->ijc", dbias_own, pair_bias_matrix, preferred_element_type=jnp.float32
    ).astype(jnp.bfloat16)
    part_bias = jnp.einsum(
        "ijc,hij->ch", pair_input_rows, dbias_own, preferred_element_type=jnp.float32
    )
    totals = lax.psum(
        (part_gain, part_query, part_key, part_value, part_gate, part_out, part_bias),
        ("seq", "res"),
    )
    return (
        alignment_rows_gradient,
        pair_input_gradient,
        totals[0],
        totals[1],
        totals[2],
        totals[3],
        totals[4],
        totals[5],
        totals[6],
    )


def solution(mesh):
    in_specs = (
        P("seq", "res", None),
        P("res", "seq", None),
        P("seq", "res", None),
        P(),
        P(),
        P(),
        P(),
        P(),
        P(),
        P(),
    )
    out_specs = (P("seq", "res", None), P("res", "seq", None), P(), P(), P(), P(), P(), P(), P())
    return jax.shard_map(body, mesh=mesh, in_specs=in_specs, out_specs=out_specs, check_vma=False)
```

profile of v0, /device:TPU:1, one launch (start us, length us, event | category | flops | bytes accessed | tf_op | source)
XLA Modules:
  0.0 668.8 jit_solution(14989727427753423162)
XLA Ops:
  7.3 6.7 convolution_convert_fusion.3
  18.7 28.2 %all-gather.5.cloned.1.call-done = bf16[8,64,2048]{2,0,1:T(8,128)(2,1)} async-done(((bf16[8,64,512]{2,0,1:T(8,128)(2,1)}), bf16[8,64,2048]{2,0,1:T(8,128)(2,1)}) %all-gather.5.cloned.1.call-update) | async-done | bytes 2097168 | tf_op jit(solution)/shard_map/all_gather | solution.py:101
  46.9 4.1 copy.34
  51.0 80.8 %all-gather.3.cloned.1.call-done = bf16[4,2048,256]{2,1,0:T(8,128)(2,1)} async-done(((bf16[4,64,256]{2,1,0:T(8,128)(2,1)}), bf16[4,2048,256]{2,1,0:T(8,128)(2,1)}) %all-gather.3.cloned.1.call-update) | async-done | bytes 4194320 | tf_op jit(solution)/shard_map/all_gather | solution.py:102
  131.8 5.6 convolution_convert_fusion
  137.4 3.2 convolution_convert_fusion.1
  140.6 105.2 %while.21 = (s32[]{:T(128)}, f32[8,64,2048]{2,1,0:T(8,128)}, bf16[4,64,256]{1,2,0:T(8,128)(2,1)}, bf16[4,64,256]{1,2,0:T(8,128)(2,1)}, bf16[4,64,256]{1,2,0:T(8,...) while((s32[]{:T(128)}, f32[8,64,2048]{2,1,0:T(8,128)}, ...), condition=%wide.region_6.7_spmd.clone, body=%wide.region_2.6_spmd.clone.sunk | while | flops 422233600 | bytes 126007688 | solution.py:116
  141.5 1.3 constant_dynamic-slice_fusion.11
  143.4 1.3 constant_dynamic-slice_fusion.9
  145.4 4.9 fusion.108
  150.3 3.1 fusion.109
  155.5 2.8 multiply_reduce_fusion.3
  158.8 3.5 fusion.111
  164.6 2.3 constant_dynamic-update-slice_fusion.10
  169.7 1.3 constant_dynamic-slice_fusion.9
  171.7 4.9 fusion.108
  176.6 3.1 fusion.109
  181.8 2.8 multiply_reduce_fusion.3
  185.1 3.5 fusion.111
  190.9 2.3 constant_dynamic-update-slice_fusion.10
  198.0 4.9 fusion.108
  202.9 3.1 fusion.109
  208.1 2.8 multiply_reduce_fusion.3
  211.4 3.5 fusion.111
  217.2 2.3 constant_dynamic-update-slice_fusion.10
  220.4 1.3 constant_dynamic-slice_fusion.11
  224.3 4.9 fusion.108
  229.2 3.1 fusion.109
  234.4 2.8 multiply_reduce_fusion.3
  237.6 3.5 fusion.111
  243.5 2.3 constant_dynamic-update-slice_fusion.10
  246.1 8.8 %copy.40 = f32[4,2048,256]{2,1,0:T(8,128)} copy(f32[4,2048,256]{1,2,0:T(8,128)} %get-tuple-element.83) | data formatting | bytes 16777216 | tf_op jit(solution)/shard_map/while | solution.py:116
  254.8 8.7 %copy.41 = f32[4,2048,256]{2,1,0:T(8,128)} copy(f32[4,2048,256]{1,2,0:T(8,128)} %get-tuple-element.84) | data formatting | bytes 16777216 | tf_op jit(solution)/shard_map/while | solution.py:116
  263.6 6.7 %fusion.38 = f32[8192,256]{1,0:T(8,128)S(1)} fusion(f32[8192,256]{1,0:T(8,128)} %bitcast.143, bf16[256,256]{1,0:T(8,128)(2,1)S(1)} %copy-done), kind=kOutput, calls=%fused_computation.79 | convolution fusion | flops 6442450944 | bytes 16908288 | tf_op jit(solution)/shard_map/dot_general | solution.py:133
  270.3 6.4 convolution_add_fusion
  281.1 11.1 %convolution_bitcast_fusion.2 = f32[256,256]{1,0:T(8,128)} fusion(bf16[4,2048,256]{2,1,0:T(8,128)(2,1)} %all-gather.3.cloned.1.call-done, f32[4,2048,256]{1,2,0:T(8,128)} %get-tuple-element.84), kind=kOutput, calls=%fused_computation.40 | convolution fusion | flops 6442450944 | bytes 12845056 | tf_op jit(solution)/shard_map/dot_general | solution.py:141
  292.2 8.4 %convolution_bitcast_fusion.3 = f32[256,256]{1,0:T(8,128)} fusion(bf16[4,2048,256]{2,1,0:T(8,128)(2,1)S(1)} %copy-done.5, f32[4,2048,256]{1,2,0:T(8,128)} %get-tuple-element.83), kind=kOutput, calls=%fused_computation.41 | convolution fusion | flops 6442450944 | bytes 12845056 | tf_op jit(solution)/shard_map/dot_general | solution.py:140
  300.6 1.3 convert_element_type.67
  301.9 4.8 convolution_bitcast_fusion.5
  306.8 5.5 convolution_convert_fusion.2
  312.4 165.3 %reduce-scatter.3.cloned.1.call-done = f32[4,64,256]{2,1,0:T(8,128)} async-done(((f32[4,2048,256]{2,1,0:T(8,128)}), f32[4,64,256]{2,1,0:T(8,128)}) %reduce-scatter.3.cloned.1.call-update) | async-done | bytes 262160 | tf_op jit(solution)/shard_map/reduce_scatter | solution.py:136
  479.2 84.4 %all-reduce = (f32[256]{0:T(256)}, f32[128,8]{0,1:T(8,128)}) all-reduce(f32[256]{0:T(256)S(1)} %get-tuple-element.155, f32[128,8]{0,1:T(8,128)S(1)} %convolution_bitcast_fusion.5), channel_id=1, replica_groups=mesh['seq'=4,'res'=32] {'seq','res'}, use_global_device_ids=true, to_apply=%region_12.13 | all-reduce | flops 1280 | bytes 10240 | tf_op jit(solution)/shard_map/psum | solution.py:177
  564.5 89.4 %all-reduce.4.cloned.1.call-done = (f32[256,256]{1,0:T(8,128)}, f32[256,256]{1,0:T(8,128)}, f32[256,256]{1,0:T(8,128)}, f32[256,256]{1,0:T(8,128)}, f32[256,256]{1,0:T(8,128)}) async-done(((f32[256,256]{1,0:T(8,128)}, f32[256,256]{1,0:T(8,128)}, f32[256,256]{1,0:T(8,128)}, f32[256,256]{1,0:T(8,128)}, f32[256,256]{1,0:T(8,128)}), (f32[256,256]{1,0:T(8,128)}, f32[256,256]{1,0:T(8,128)}, f32[256,256]{1,0:T(8,128)}, ...) | async-done | bytes 1310736 | tf_op jit(solution)/shard_map/psum | solution.py:177
  653.9 1.7 copy.102
  655.6 1.7 copy.103
  657.3 1.7 copy.104
  658.9 1.7 copy.105
  660.6 1.7 copy.106
  (197 shorter events, 44.8 us)
Async XLA Ops:
  7.2 130.2 %copy-start = (bf16[256,256]{1,0:T(8,128)(2,1)S(1)}, bf16[256,256]{1,0:T(8,128)(2,1)}, u32[]{:S(2)}) copy-start(bf16[256,256]{1,0:T(8,128)(2,1)} %param.17) | copy-start | bytes 393220
  7.2 6.9 %copy-start.8 = (bf16[4,64,256]{2,1,0:T(8,128)(2,1)S(1)}, bf16[4,64,256]{2,1,0:T(8,128)(2,1)}, u32[]{:S(2)}) copy-start(bf16[4,64,256]{2,1,0:T(8,128)(2,1)} %param.12) | copy-start | bytes 393220
  7.2 7.2 %copy-start.30 = (f32[256]{0:T(256)S(1)}, f32[256]{0:T(256)}, u32[]{:S(2)}) copy-start(f32[256]{0:T(256)} %param.15) | copy-start | bytes 3076
  7.2 8.2 %copy-start.18 = (bf16[256,256]{1,0:T(8,128)(2,1)S(1)}, bf16[256,256]{1,0:T(8,128)(2,1)}, u32[]{:S(2)}) copy-start(bf16[256,256]{1,0:T(8,128)(2,1)} %param.16) | copy-start | bytes 393220
  7.2 9.3 %copy-start.24 = (bf16[256,256]{1,0:T(8,128)(2,1)S(1)}, bf16[256,256]{1,0:T(8,128)(2,1)}, u32[]{:S(2)}) copy-start(bf16[256,256]{1,0:T(8,128)(2,1)} %param.19) | copy-start | bytes 393220
  7.2 10.4 %copy-start.16 = (bf16[4,64,256]{2,1,0:T(8,128)(2,1)S(1)}, bf16[4,64,256]{2,1,0:T(8,128)(2,1)}, u32[]{:S(2)}) copy-start(bf16[4,64,256]{2,1,0:T(8,128)(2,1)} %param.14) | copy-start | bytes 393220
  7.3 10.4 %copy-start.23 = (bf16[256,256]{1,0:T(8,128)(2,1)S(1)}, bf16[256,256]{1,0:T(8,128)(2,1)}, u32[]{:S(2)}) copy-start(bf16[256,256]{1,0:T(8,128)(2,1)} %param.20) | copy-start | bytes 393220
  7.3 39.7 %all-gather.5.cloned.1.call-start = ((), (), s32[]{:S(2)}) async-start(), calls=%async_computation.3 | async-start | bytes 2621440 | tf_op jit(solution)/shard_map/all_gather | solution.py:101
  14.0 117.8 %copy-start.14 = (bf16[256,256]{1,0:T(8,128)(2,1)S(1)}, bf16[256,256]{1,0:T(8,128)(2,1)}, u32[]{:S(2)}) copy-start(bf16[256,256]{1,0:T(8,128)(2,1)} %param.18) | copy-start | bytes 393220
  14.0 117.8 %all-gather.3.cloned.1.call-start = ((), (), s32[]{:S(2)}) async-start(), calls=%async_computation.2 | async-start | bytes 4325376 | tf_op jit(solution)/shard_map/all_gather | solution.py:102
  14.2 1.2 copy-start.26
  15.3 285.4 %reduce-scatter.5.cloned.1.call-start = ((), (), s32[]{:S(2)}) async-start(), calls=%async_computation.5 | async-start | bytes 5242880 | tf_op jit(solution)/shard_map/reduce_scatter | solution.py:168
  131.8 5.6 copy-start.4
  150.3 4.7 copy-start.1
  155.5 3.2 copy-start.2
  162.3 4.6 copy-start.3
  164.6 2.3 copy-start.13
  164.6 2.3 copy-start.21
  176.6 4.7 copy-start.1
  181.8 3.2 copy-start.2
  188.6 4.6 copy-start.3
  190.9 2.3 copy-start.13
  190.9 2.3 copy-start.21
  202.9 4.7 copy-start.1
  208.1 3.2 copy-start.2
  214.9 4.6 copy-start.3
  217.2 2.3 copy-start.13
  217.2 2.3 copy-start.21
  229.2 4.7 copy-start.1
  234.4 3.2 copy-start.2
  241.2 4.6 copy-start.3
  243.5 2.3 copy-start.13
  243.5 2.3 copy-start.21
  245.8 231.8 %reduce-scatter.3.cloned.1.call-start = ((), (), s32[]{:S(2)}) async-start(), calls=%async_computation.4 | async-start | bytes 8650752 | tf_op jit(solution)/shard_map/reduce_scatter | solution.py:136
  263.6 6.7 %copy-start.6 = (f32[4,2048,256]{2,1,0:T(8,128)S(1)}, f32[4,2048,256]{2,1,0:T(8,128)}, u32[]{:S(2)}) copy-start(f32[4,2048,256]{2,1,0:T(8,128)} %copy.41) | copy-start | bytes 25165828
  263.6 6.7 %copy-start.15 = (bf16[256,256]{1,0:T(8,128)(2,1)S(1)}, bf16[256,256]{1,0:T(8,128)(2,1)}, u32[]{:S(2)}) copy-start(bf16[256,256]{1,0:T(8,128)(2,1)} %param.18) | copy-start | bytes 393220
  276.7 1.2 copy-start.7
  276.7 3.2 copy-start.17
  276.7 3.2 copy-start.22
  276.7 4.1 copy-start.19
  276.8 377.2 %all-reduce.4.cloned.1.call-start = ((), (), s32[]{:S(2)}) async-start(), calls=%async_computation.6 | async-start | bytes 2621440 | tf_op jit(solution)/shard_map/psum | solution.py:177
  281.1 11.1 %copy-start.5 = (bf16[4,2048,256]{2,1,0:T(8,128)(2,1)S(1)}, bf16[4,2048,256]{2,1,0:T(8,128)(2,1)}, u32[]{:S(2)}) copy-start(bf16[4,2048,256]{2,1,0:T(8,128)(2,1)} %all-gather.3.cloned.1.call-done) | copy-start | bytes 12582916
  301.9 4.8 copy-start.32
  306.8 170.9 %copy-start.25 = (bf16[256,256]{1,0:T(8,128)(2,1)S(1)}, bf16[256,256]{1,0:T(8,128)(2,1)}, u32[]{:S(2)}) copy-start(bf16[256,256]{1,0:T(8,128)(2,1)} %param.19) | copy-start | bytes 393220
  306.8 170.9 %copy-start.31 = (f32[256]{0:T(256)S(1)}, f32[256]{0:T(256)}, u32[]{:S(2)}) copy-start(f32[256]{0:T(256)} %param.15) | copy-start | bytes 3076
  306.8 172.2 %copy-start.9 = (bf16[4,64,256]{2,1,0:T(8,128)(2,1)S(1)}, bf16[4,64,256]{2,1,0:T(8,128)(2,1)}, u32[]{:S(2)}) copy-start(bf16[4,64,256]{2,1,0:T(8,128)(2,1)} %param.12) | copy-start | bytes 393220
  306.8 172.2 %copy-start.27 = (f32[4,64]{1,0:T(4,128)S(1)}, f32[4,64]{1,0:T(4,128)}, u32[]{:S(2)}) copy-start(f32[4,64]{1,0:T(4,128)} %copy-done.26) | copy-start | bytes 3076
  306.8 172.2 %copy-start.29 = (f32[4,64]{1,0:T(4,128)S(1)}, f32[4,64]{1,0:T(4,128)}, u32[]{:S(2)}) copy-start(f32[4,64]{1,0:T(4,128)} %copy-done.28) | copy-start | bytes 3076
  (11 other events, 8.6 us)
Sparse Core Ops, SparseCore 0:
  14.1 32.7 all-gather.4
  50.6 81.1 all-gather.2
  246.0 44.0 reduce-scatter.4
  292.3 185.3 reduce-scatter.2
  483.8 170.0 all-reduce.3
where the time goes:
time: 670 us; the launch traced here: 669 us
  waiting for transfers between devices  364 us (54%)
  matrix products  116 us (17%)
  blocking collectives  84.4 us (13%)
  local copies, waits for them, and re-layouts  68.2 us (10%)
  other arithmetic  21.5 us (3%)
  between operations  14.2 us (2%)
    reduce_scatter x1, waiting for transfers between devices, body(): lax.psum_scatter(key_term, 'res', scatter_dimension=1, tiled=True)  165 us
    psum x1, waiting for transfers between devices, body(): lax.psum((part_gain, part_query, part_key, part_value, part_gate, part_ou...  89.4 us
    psum x1, blocking collectives, body(): lax.psum((part_gain, part_query, part_key, part_value, part_gate, part_ou...  84.4 us
    all_gather x1, waiting for transfers between devices, body(): normed_all = lax.all_gather(rescaled_embedding, 'res', axis=1, tiled=True)  80.8 us
    all_gather x1, waiting for transfers between devices, body(): bias_full = lax.all_gather(bias_local, 'seq', axis=2, tiled=True)  28.2 us
    sub x4, matrix products, row_backward(): weights_soft = jax.nn.softmax(scores, axis=-1)  19.8 us
    while x4, local copies, waits for them, and re-layouts, body(): lax.scan(functools.partial(row_backward, bias_full, head_count), dbias_in...  17.7 us
    dynamic_slice x32, local copies, waits for them, and re-layouts, body(): lax.scan(functools.partial(row_backward, bias_full, head_count), dbias_in...  16.4 us
  transfers between devices with their start and end apart: 5, of which 4 were waited for; matrix products, arithmetic and copies ran while one was open for 11% of the time, Pallas kernels for 0%

commit v1 on v0

--- a/solution.py
+++ b/solution.py
@@ -175,8 +175,10 @@
         "ijc,hij->ch", pair_input_rows, dbias_own, preferred_element_type=jnp.float32
     )
     totals = lax.psum(
-        (part_gain, part_query, part_key, part_value, part_gate, part_out, part_bias),
-        ("seq", "res"),
+        lax.psum(
+            (part_gain, part_query, part_key, part_value, part_gate, part_out, part_bias), "res"
+        ),
+        "seq",
     )
     return (
         alignment_rows_gradient,

time: 670 us -> 1000 us (1.49)
  waiting for transfers between devices: 364 us -> 657 us
  blocking collectives: 84.4 us -> 121 us
    psum x1, waiting for transfers between devices: 89.4 us -> 299 us  [body(): lax.psum((part_gain, part_query, part_key, part_value, part_gate, part_ou...]
    reduce_scatter x1, waiting for transfers between devices: 0.02 us -> 71.2 us  [body(): lax.psum_scatter(dbias_local, 'seq', scatter_dimension=2, tiled=True)]
    psum x0 -> x1, blocking collectives: none -> 41.3 us  [body(): lax.psum(lax.psum((part_gain, part_query, part_key, part_value, part_gate...]
    reduce_scatter x1, waiting for transfers between devices: 165 us -> 177 us  [body(): lax.psum_scatter(key_term, 'res', scatter_dimension=1, tiled=True)]
  transfers between devices with their start and end apart: 5 -> 6, of which waited for: 4 -> 5; matrix products, arithmetic and copies ran while one was open for 11% -> 5% of each run, Pallas kernels for 0% -> 0%
where the time goes in v1:
time: 1000 us; the launch traced here: 999 us
  waiting for transfers between devices  657 us (66%)
  blocking collectives  121 us (12%)
  matrix products  116 us (12%)
  local copies, waits for them, and re-layouts  68.3 us (7%)
  other arithmetic  21.5 us (2%)
  between operations  14.5 us (1%)
    psum x1, waiting for transfers between devices, body(): lax.psum((part_gain, part_query, part_key, part_value, part_gate, part_ou...  299 us
    reduce_scatter x1, waiting for transfers between devices, body(): lax.psum_scatter(key_term, 'res', scatter_dimension=1, tiled=True)  177 us
    all_gather x1, waiting for transfers between devices, body(): normed_all = lax.all_gather(rescaled_embedding, 'res', axis=1, tiled=True)  80.8 us
    psum x1, blocking collectives, body(): lax.psum((part_gain, part_query, part_key, part_value, part_gate, part_ou...  79.5 us
    reduce_scatter x1, waiting for transfers between devices, body(): lax.psum_scatter(dbias_local, 'seq', scatter_dimension=2, tiled=True)  71.2 us
    psum x1, blocking collectives, body(): lax.psum(lax.psum((part_gain, part_query, part_key, part_value, part_gate...  41.3 us
    all_gather x1, waiting for transfers between devices, body(): bias_full = lax.all_gather(bias_local, 'seq', axis=2, tiled=True)  28.2 us
  transfers between devices with their start and end apart: 6, of which 5 were waited for; matrix products, arithmetic and copies ran while one was open for 5% of the time, Pallas kernels for 0%

profile of v1, /device:TPU:1, one launch (start us, length us, event | category | flops | bytes accessed | tf_op | source)
XLA Modules:
  0.0 999.2 jit_solution(7296195740414935652)
XLA Ops:
  7.3 6.7 convolution_convert_fusion.3
  18.7 28.2 %all-gather.5.cloned.1.call-done = bf16[8,64,2048]{2,0,1:T(8,128)(2,1)} async-done(((bf16[8,64,512]{2,0,1:T(8,128)(2,1)}), bf16[8,64,2048]{2,0,1:T(8,128)(2,1)}) %all-gather.5.cloned.1.call-update) | async-done | bytes 2097168 | tf_op jit(solution)/shard_map/all_gather | solution.py:101
  46.9 4.1 copy.34
  51.0 80.8 %all-gather.3.cloned.1.call-done = bf16[4,2048,256]{2,1,0:T(8,128)(2,1)} async-done(((bf16[4,64,256]{2,1,0:T(8,128)(2,1)}), bf16[4,2048,256]{2,1,0:T(8,128)(2,1)}) %all-gather.3.cloned.1.call-update) | async-done | bytes 4194320 | tf_op jit(solution)/shard_map/all_gather | solution.py:102
  131.8 5.5 convolution_convert_fusion
  137.3 3.2 convolution_convert_fusion.1
  140.5 105.6 %while.21 = (s32[]{:T(128)}, f32[8,64,2048]{2,1,0:T(8,128)}, bf16[4,64,256]{1,2,0:T(8,128)(2,1)}, bf16[4,64,256]{1,2,0:T(8,128)(2,1)}, bf16[4,64,256]{1,2,0:T(8,...) while((s32[]{:T(128)}, f32[8,64,2048]{2,1,0:T(8,128)}, ...), condition=%wide.region_6.7_spmd.clone, body=%wide.region_2.6_spmd.clone.sunk | while | flops 422233600 | bytes 126007688 | solution.py:116
  145.3 5.0 fusion.108
  150.2 3.1 fusion.109
  155.5 2.8 multiply_reduce_fusion.3
  158.7 3.5 fusion.111
  164.6 2.3 constant_dynamic-update-slice_fusion.10
  171.6 5.0 fusion.108
  176.6 3.1 fusion.109
  181.8 2.8 multiply_reduce_fusion.3
  185.1 3.5 fusion.111
  190.9 2.3 constant_dynamic-update-slice_fusion.10
  198.0 5.0 fusion.108
  203.0 3.1 fusion.109
  208.2 2.8 multiply_reduce_fusion.3
  211.4 3.5 fusion.111
  217.3 2.3 constant_dynamic-update-slice_fusion.10
  224.3 5.0 fusion.108
  229.3 3.1 fusion.109
  234.5 2.8 multiply_reduce_fusion.3
  237.8 3.5 fusion.111
  243.6 2.3 constant_dynamic-update-slice_fusion.10
  246.1 2.0 convolution_bitcast_fusion.1
  248.1 2.0 convolution_bitcast_fusion.4
  250.1 1.9 convolution_bitcast_fusion
  252.0 10.9 %convolution_bitcast_fusion.2 = f32[256,256]{1,0:T(8,128)} fusion(bf16[4,2048,256]{2,1,0:T(8,128)(2,1)} %all-gather.3.cloned.1.call-done, f32[4,2048,256]{1,2,0:T(8,128)} %get-tuple-element.84), kind=kOutput, calls=%fused_computation.40 | convolution fusion | flops 6442450944 | bytes 12845056 | tf_op jit(solution)/shard_map/dot_general | solution.py:141
  262.9 6.1 convolution_bitcast_fusion.3
  269.7 9.0 copy.40
  278.7 8.7 copy.41
  287.3 6.6 fusion.38
  294.0 6.4 convolution_add_fusion
  301.9 298.5 %all-reduce.7.cloned.1.call-done = (f32[256,256]{1,0:T(8,128)}, f32[256,256]{1,0:T(8,128)}, f32[256,256]{1,0:T(8,128)}, f32[256,256]{1,0:T(8,128)}, f32[256,256]{1,0:T(8,128)}) async-done(((f32[256,256]{1,0:T(8,128)}, f32[256,256]{1,0:T(8,128)}, f32[256,256]{1,0:T(8,128)}, f32[256,256]{1,0:T(8,128)}, f32[256,256]{1,0:T(8,128)}), (f32[256,256]{1,0:T(8,128)}, f32[256,256]{1,0:T(8,128)}, f32[256,256]{1,0:T(8,128)}, ...) | async-done | bytes 1310736 | tf_op jit(solution)/shard_map/psum | solution.py:178
  600.4 71.2 %reduce-scatter.5.cloned.1.call-done = f32[8,64,512]{2,1,0:T(8,128)} async-done(((f32[8,64,2048]{2,1,0:T(8,128)}), f32[8,64,512]{2,1,0:T(8,128)}) %reduce-scatter.5.cloned.1.call-update) | async-done | bytes 1048592 | tf_op jit(solution)/shard_map/reduce_scatter | solution.py:168
  673.0 4.8 convolution_bitcast_fusion.5
  677.9 5.5 convolution_convert_fusion.2
  683.4 177.4 %reduce-scatter.3.cloned.1.call-done = f32[4,64,256]{2,1,0:T(8,128)} async-done(((f32[4,2048,256]{2,1,0:T(8,128)}), f32[4,64,256]{2,1,0:T(8,128)}) %reduce-scatter.3.cloned.1.call-update) | async-done | bytes 262160 | tf_op jit(solution)/shard_map/reduce_scatter | solution.py:136
  862.4 79.5 %all-reduce = (f32[256]{0:T(256)S(1)}, f32[128,8]{0,1:T(8,128)S(1)}) all-reduce(f32[256]{0:T(256)S(1)} %get-tuple-element.155, f32[128,8]{0,1:T(8,128)S(1)} %convolution_bitcast_fusion.5), channel_id=1, replica_groups=mesh['seq'=4,'res'=32] {'res'}, use_global_device_ids=true, to_apply=%region_12.13 | all-reduce | flops 1280 | bytes 10240 | tf_op jit(solution)/shard_map/psum | solution.py:178
  941.8 41.3 %all-reduce.2 = (f32[256]{0:T(256)}, f32[128,8]{0,1:T(8,128)}) all-reduce(f32[256]{0:T(256)S(1)} %get-tuple-element.183, f32[128,8]{0,1:T(8,128)S(1)} %get-tuple-element.184), channel_id=1, replica_groups=mesh['seq'=4,'res'=32] {'seq'}, use_global_device_ids=true, to_apply=%region_13.14 | all-reduce | flops 1280 | bytes 10240 | tf_op jit(solution)/shard_map/psum | solution.py:177
  984.0 1.7 copy.107
  985.7 1.7 copy.108
  987.3 1.7 copy.109
  989.0 1.7 copy.110
  990.7 1.7 copy.111
  (197 shorter events, 48.7 us)
Async XLA Ops:
  7.2 130.2 %copy-start = (bf16[256,256]{1,0:T(8,128)(2,1)S(1)}, bf16[256,256]{1,0:T(8,128)(2,1)}, u32[]{:S(2)}) copy-start(bf16[256,256]{1,0:T(8,128)(2,1)} %param.17) | copy-start | bytes 393220
  7.2 6.9 copy-start.8
  7.2 7.2 copy-start.28
  7.2 8.2 copy-start.17
  7.2 9.3 copy-start.22
  7.2 10.4 %copy-start.16 = (bf16[4,64,256]{2,1,0:T(8,128)(2,1)S(1)}, bf16[4,64,256]{2,1,0:T(8,128)(2,1)}, u32[]{:S(2)}) copy-start(bf16[4,64,256]{2,1,0:T(8,128)(2,1)} %param.14) | copy-start | bytes 393220
  7.3 10.4 %copy-start.21 = (bf16[256,256]{1,0:T(8,128)(2,1)S(1)}, bf16[256,256]{1,0:T(8,128)(2,1)}, u32[]{:S(2)}) copy-start(bf16[256,256]{1,0:T(8,128)(2,1)} %param.20) | copy-start | bytes 393220
  7.3 39.7 %all-gather.5.cloned.1.call-start = ((), (), s32[]{:S(2)}) async-start(), calls=%async_computation.3 | async-start | bytes 2621440 | tf_op jit(solution)/shard_map/all_gather | solution.py:101
  14.0 117.8 %copy-start.14 = (bf16[256,256]{1,0:T(8,128)(2,1)S(1)}, bf16[256,256]{1,0:T(8,128)(2,1)}, u32[]{:S(2)}) copy-start(bf16[256,256]{1,0:T(8,128)(2,1)} %param.18) | copy-start | bytes 393220
  14.0 117.8 %all-gather.3.cloned.1.call-start = ((), (), s32[]{:S(2)}) async-start(), calls=%async_computation.2 | async-start | bytes 4325376 | tf_op jit(solution)/shard_map/all_gather | solution.py:102
  14.2 1.2 copy-start.24
  15.2 585.2 %all-reduce.7.cloned.1.call-start = ((), (), s32[]{:S(2)}) async-start(), calls=%async_computation.6 | async-start | bytes 2621440 | tf_op jit(solution)/shard_map/psum | solution.py:178
  131.8 5.5 copy-start.4
  150.2 4.7 copy-start.1
  155.5 3.2 copy-start.2
  162.2 4.6 copy-start.3
  164.5 2.3 copy-start.13
  164.6 2.3 copy-start.20
  176.6 4.7 copy-start.1
  181.8 3.2 copy-start.2
  188.6 4.6 copy-start.3
  190.9 2.3 copy-start.13
  190.9 2.3 copy-start.20
  202.9 4.7 copy-start.1
  208.2 3.2 copy-start.2
  214.9 4.6 copy-start.3
  217.2 2.3 copy-start.13
  217.2 2.3 copy-start.20
  229.3 4.7 copy-start.1
  234.5 3.2 copy-start.2
  241.3 4.6 copy-start.3
  243.6 2.3 copy-start.13
  243.6 2.3 copy-start.20
  252.0 10.9 %copy-start.5 = (bf16[4,2048,256]{2,1,0:T(8,128)(2,1)S(1)}, bf16[4,2048,256]{2,1,0:T(8,128)(2,1)}, u32[]{:S(2)}) copy-start(bf16[4,2048,256]{2,1,0:T(8,128)(2,1)} %all-gather.3.cloned.1.call-done) | copy-start | bytes 12582916
  252.0 10.9 %copy-start.7 = (f32[4,2048,256]{1,2,0:T(8,128)S(1)}, f32[4,2048,256]{1,2,0:T(8,128)}, u32[]{:S(2)}) copy-start(f32[4,2048,256]{1,2,0:T(8,128)} %get-tuple-element.83) | copy-start | bytes 25165828
  269.1 402.6 %reduce-scatter.5.cloned.1.call-start = ((), (), s32[]{:S(2)}) async-start(), calls=%async_computation.5 | async-start | bytes 5242880 | tf_op jit(solution)/shard_map/reduce_scatter | solution.py:168
  269.7 591.1 %reduce-scatter.3.cloned.1.call-start = ((), (), s32[]{:S(2)}) async-start(), calls=%async_computation.4 | async-start | bytes 8650752 | tf_op jit(solution)/shard_map/reduce_scatter | solution.py:136
  287.3 6.7 copy-start.6
  287.3 6.7 copy-start.15
  300.4 1.1 copy-start.10
  300.4 1.2 copy-start.18
  300.5 683.5 %all-reduce.9.cloned.1.call-start = ((), (), s32[]{:S(2)}) async-start(), calls=%async_computation.7 | async-start | bytes 2621440 | tf_op jit(solution)/shard_map/psum | solution.py:177
  673.0 4.8 copy-start.30
  677.8 183.0 %copy-start.23 = (bf16[256,256]{1,0:T(8,128)(2,1)S(1)}, bf16[256,256]{1,0:T(8,128)(2,1)}, u32[]{:S(2)}) copy-start(bf16[256,256]{1,0:T(8,128)(2,1)} %param.19) | copy-start | bytes 393220
  677.8 183.0 %copy-start.29 = (f32[256]{0:T(256)S(1)}, f32[256]{0:T(256)}, u32[]{:S(2)}) copy-start(f32[256]{0:T(256)} %param.15) | copy-start | bytes 3076
  677.8 184.3 %copy-start.9 = (bf16[4,64,256]{2,1,0:T(8,128)(2,1)S(1)}, bf16[4,64,256]{2,1,0:T(8,128)(2,1)}, u32[]{:S(2)}) copy-start(bf16[4,64,256]{2,1,0:T(8,128)(2,1)} %param.12) | copy-start | bytes 393220
  677.8 184.3 %copy-start.25 = (f32[4,64]{1,0:T(4,128)S(1)}, f32[4,64]{1,0:T(4,128)}, u32[]{:S(2)}) copy-start(f32[4,64]{1,0:T(4,128)} %copy-done.24) | copy-start | bytes 3076
  677.8 184.3 %copy-start.27 = (f32[4,64]{1,0:T(4,128)S(1)}, f32[4,64]{1,0:T(4,128)}, u32[]{:S(2)}) copy-start(f32[4,64]{1,0:T(4,128)} %copy-done.26) | copy-start | bytes 3076
  (10 other events, 7.5 us)
Sparse Core Ops, SparseCore 0:
  14.1 32.7 all-gather.4
  50.6 81.1 all-gather.2
  269.2 331.1 all-reduce.6
  602.7 68.9 reduce-scatter.4
  673.9 186.8 reduce-scatter.2
  863.5 65.2 all-reduce.8
